TPU v7x, 128 devices: a whole 4x4x4 slice. The times are simulated.
128 devices in a mesh: dom: 128 (over x, y, z, core).
Axes of the slice: x: 4, y: 4, z: 4, core: 2. Of those that a mesh axis runs over, the one named last changes fastest.
Arguments:
- adjoint: float32 [4, 8, 64, 32768], P(None, None, None, 'dom'), may hold values from -1.5 to 1.5
- velocity: bfloat16 [3, 64, 32768], P(None, None, 'dom'), may hold values from -4 to 4
- metric: float32 [3, 32768], P(None, 'dom'), may hold values from 0.5 to 2
- face_scale: float32 [6, 32768], P(None, 'dom'), may hold values from 0.5 to 2
- resistance: float32 [2, 1024], P(None, 'dom'), may hold values from 0.5 to 2
- elem_count: int32 [128], P('dom'), may hold values from 192 to 256, as said below
- face_partner: int32 [6, 32768], P(None, 'dom'), may hold values from -1 to 1535, as said below
- link_face: int32 [128, 7, 32], P('dom'), may hold values from -1 to 1535, as said below
- outlet_face: int32 [128, 32], P('dom'), may hold values from 0 to 1535, as said below
- outlet_id: int32 [128, 32], P('dom'), may hold values from 0 to 1023, as said below
Outputs:
- adj_res: float32 [4, 8, 64, 32768], P(None, None, None, 'dom')
- multiplier: float32 [8, 1024], P(None, 'dom')
Inputs may be any that keep to these rules, and one draw needn't show every extreme that they name: Elements e >= elem_count[p] of device p are padding. Some device uses all 256. `face_partner`: values are local face ids of the same device or -1. The relation is symmetric, never pairs a face with itself, names only faces of used elements, and forms exactly 256 pairs on each device. Faces named in link_face or outlet_face have -1. link_face[p][b][s] is a local face id of a used element of device p, or -1 exactly when s is at least the count of the pair of devices p and p XOR 2^b, a count shared by both and at least 16. For every b some pair uses all 32 slots. Used entries are distinct on a device and are not outlet faces. `outlet_face`: 32 distinct local face ids of used elements on each device. `outlet_id`: over all devices every outlet is named exactly 4 times.
All inputs are finite; a program needn't handle non-finite values.
Results may differ from a plain program's by a relative error of at most 0.0003.
Values sent between devices are 32-bit elements; how exact they have to be, the bound alone decides.
No kernel may reach another device: no remote copies, remote signals or barrier semaphores. Data moves between devices by JAX's collectives and lax.ppermute only.
A program may use at most 256 MiB of HBM per device.

v0:
```python
import math

import jax
import jax.numpy as jnp
import numpy as np
from jax import lax
from jax.experimental import pallas as pl
from jax.experimental.pallas import tpu as pltpu
from jax.sharding import PartitionSpec as P


F32 = jnp.float32
BF16 = jnp.bfloat16
VISCOUS = 0.05
PENALTY = 1.0
COMPS, OBJ, NODES, ELEMS = 4, 8, 64, 256
LANES = 128
CAP, LEVELS = 32, 7
FACE_ROWS = COMPS * CAP
MSG = 4
HIGHEST = lax.Precision.HIGHEST


def gll_tables():
    root_five = math.sqrt(5.0)
    points = np.array([-1.0, -1.0 / root_five, 1.0 / root_five, 1.0])
    weights = np.array([1.0, 5.0, 5.0, 1.0]) / 6.0
    products = np.array(
        [np.prod([points[i] - points[k] for k in range(4) if k != i]) for i in range(4)]
    )
    derivative = np.zeros((4, 4))
    for i in range(4):
        for j in range(4):
            if i != j:
                derivative[i, j] = products[i] / (products[j] * (points[i] - points[j]))
        derivative[i, i] = -np.sum(derivative[i])
    return (derivative, weights)


DERIV, WEIGHTS = gll_tables()
FACE_W = np.outer(WEIGHTS, WEIGHTS).reshape(16)


def split3(array):
    high = np.asarray(array, np.float32).astype(jnp.bfloat16)
    rest = np.asarray(array, np.float32) - high.astype(np.float32)
    middle = rest.astype(jnp.bfloat16)
    low = (rest - middle.astype(np.float32)).astype(jnp.bfloat16)
    return high, middle, low


def node_matrices():
    identity = np.eye(4)
    return np.concatenate(
        [
            np.kron(DERIV, np.kron(identity, identity)),
            np.kron(identity, np.kron(DERIV, identity)),
            np.kron(identity, np.kron(identity, DERIV)),
        ]
    )


def face_node(face, m):
    axis, layer = face // 2, 3 * (face % 2)
    a, b = m // 4, m % 4
    digits = [a, b]
    digits.insert(axis, layer)
    return 16 * digits[0] + 4 * digits[1] + digits[2]


def flow_matrix():
    table = np.zeros((3, 16, NODES), np.float32)
    for face in range(6):
        row = np.zeros(NODES)
        for m in range(16):
            row[face_node(face, m)] = FACE_W[m] * (2 * (face % 2) - 1)
        for part, values in enumerate(split3(row)):
            table[face // 2, 8 * (face % 2) + part] = values.astype(np.float32)
    return table.reshape(48, NODES)


def lane_slice(half):
    return slice(half * LANES, (half + 1) * LANES)


def slot_columns(link_ref, outlet_ref, square):
    square[...] = jnp.full((LANES, LANES), -1.0, F32)
    for level in range(LEVELS):
        square[level : level + 1, 0:CAP] = link_ref[level].astype(F32)
    square[LEVELS : LEVELS + 1, 0:CAP] = outlet_ref[...].astype(F32)
    turned = jnp.transpose(square[...])
    return jnp.concatenate(
        [
            jnp.broadcast_to(turned[0:CAP, b : b + 1], (CAP, LANES))
            for b in range(LEVELS + 1)
        ],
        axis=0,
    )


def one_hot(columns, face):
    lane = lax.broadcasted_iota(jnp.int32, columns.shape, 1).astype(F32)
    parts = [
        jnp.where(columns == lane + float(face * ELEMS + half * LANES), 1.0, 0.0)
        for half in range(2)
    ]
    return jnp.concatenate(parts, axis=1).astype(BF16)


def split2(value):
    high = value.astype(BF16)
    return high, (value - high.astype(F32)).astype(BF16)


def node_major(x_ref, work_ref, comp):
    for high in range(8):
        for half in range(2):
            block = jnp.stack(
                [
                    x_ref[pl.ds(((comp * OBJ + o) * 8 + high) * 16 + half * 8, 8), :]
                    for o in range(OBJ)
                ]
            )
            start = acc_rows(comp, high * 8, half).start
            work_ref[pl.ds(start, 64), :] = jnp.swapaxes(block, 0, 1).reshape(64, LANES)


def comp_traces(work_ref, comp):
    for face in range(6):
        for m in range(0, 16, 2):
            row = (comp * 16 + m) * OBJ
            for half in range(2):
                pair = jnp.concatenate(
                    [work_ref[acc_rows(comp, face_node(face, m + i), half), :] for i in range(2)],
                    axis=0,
                )
                yield face, row, half, split2(pair)


def fill_traces(work_ref, traces, comp):
    for face, row, half, (high, low) in comp_traces(work_ref, comp):
        cols = slice(face * ELEMS + half * LANES, face * ELEMS + (half + 1) * LANES)
        traces[row : row + 16, cols] = high
        traces[512 + row : 528 + row, cols] = low


def fill_pick(pick, row):
    sub = lax.broadcasted_iota(jnp.int32, (ELEMS, row.shape[1]), 0).astype(F32)
    for face in range(6):
        pick[face * ELEMS : (face + 1) * ELEMS, :] = jnp.where(
            sub == row - float(face * ELEMS), 1.0, 0.0
        ).astype(BF16)


def parts3(value):
    high = value.astype(BF16).astype(F32)
    rest = value - high
    middle = rest.astype(BF16).astype(F32)
    return high, middle, rest - middle


def gather_kernel(
    x_any, vel_any, scale_any, link_any, outlet_any, ids_any, res_any, flow_any, count_any,
    message_ref, live_ref,
    s0_ref, s1_ref, s2_ref, s3_ref, s4_ref, s5_ref, s6_ref,
    x_ref, vel_ref, scale_ref, link_ref, outlet_ref, ids_ref, res_ref, flow_ref, count_ref,
    work_ref, traces, pick, square, total, sems,
):
    small = (
        (link_any, link_ref), (outlet_any, outlet_ref), (vel_any, vel_ref),
        (scale_any, scale_ref), (flow_any, flow_ref), (ids_any, ids_ref), (res_any, res_ref),
        (count_any, count_ref),
    )
    copies = [
        pltpu.make_async_copy(src, dst, sems.at[4 + i]) for i, (src, dst) in enumerate(small)
    ]
    blocks = [
        pltpu.make_async_copy(
            x_any.at[pl.ds(c * 1024, 1024), :], x_ref.at[pl.ds(c * 1024, 1024), :], sems.at[c]
        )
        for c in range(COMPS)
    ]
    for copy in blocks + copies:
        copy.start()
    for copy in copies:
        copy.wait()
    element = lax.broadcasted_iota(jnp.int32, (8, ELEMS), 1)
    live_ref[...] = jnp.where(element < count_ref[...], 1.0, 0.0)
    square[0:8, :] = jnp.zeros((8, LANES), F32)
    for level in range(LEVELS):
        square[level : level + 1, 0:CAP] = link_ref[level].astype(F32)
    square[LEVELS : LEVELS + 1, 0:CAP] = outlet_ref[...].astype(F32)
    head = square[0:8, :]
    pieces = [
        (pltpu.roll(head, CAP * (b % 4), 1) if b % 4 else head)[b : b + 1] for b in range(8)
    ]
    row = jnp.concatenate([sum(pieces[1:4], pieces[0]), sum(pieces[5:], pieces[4])], axis=1)
    fill_pick(pick, row)
    kind = lax.broadcasted_iota(jnp.int32, (16, ELEMS), 0)
    for face in range(6):
        axis, sign = face // 2, 2.0 * (face % 2) - 1.0
        if face % 2 == 0:
            flows = jnp.dot(
                flow_ref[16 * axis : 16 * axis + 16, :], vel_ref[axis],
                preferred_element_type=F32,
            )
        scale = scale_ref[face : face + 1, :]
        first = 8 * (face % 2)
        flow = (flows[first : first + 1] + flows[first + 1 : first + 2]) + flows[
            first + 2 : first + 3
        ]
        table = jnp.where(kind == 6, float(axis), 0.0)
        for i, part in enumerate(parts3(scale * sign) + parts3(flow * scale)):
            table = jnp.where(kind == i, part, table)
        traces[1024:1040, face * ELEMS : (face + 1) * ELEMS] = table.astype(BF16)
    for comp in range(COMPS):
        blocks[comp].wait()
        node_major(x_ref, work_ref, comp)
        fill_traces(work_ref, traces, comp)
    both = jnp.dot(traces[...], pick[...], preferred_element_type=F32)
    chosen = both[:512] + both[512:1024]
    for comp in range(COMPS):
        for half in range(2):
            total[lane_slice(half), lane_slice(comp)] = jnp.transpose(
                chosen[lane_slice(comp), lane_slice(half)]
            )
    stats = both[1024:1040, LANES:]
    square[...] = jnp.zeros((LANES, LANES), F32)
    square[0:1, :] = (stats[0:1] + stats[1:2]) + stats[2:3]
    square[1:2, :] = (stats[3:4] + stats[4:5]) + stats[5:6]
    square[2:3, :] = stats[6:7]
    stats = jnp.transpose(square[...])[LANES - CAP :]
    homes = (s0_ref, s1_ref, s2_ref, s3_ref, s4_ref, s5_ref, s6_ref)
    for level, ref in enumerate(homes):
        for comp in range(COMPS):
            ref[comp * CAP : (comp + 1) * CAP, :] = total[
                level * CAP : (level + 1) * CAP, comp * LANES : (comp + 1) * LANES
            ]
    lane = lax.broadcasted_iota(jnp.int32, (CAP, LANES), 1)
    axis = jnp.broadcast_to(stats[:, 2:3], (CAP, LANES))
    moment = jnp.zeros((CAP, LANES), F32)
    for comp in range(3):
        moment += jnp.where(
            axis == float(comp), total[LEVELS * CAP :, comp * LANES : (comp + 1) * LANES], 0.0
        )
    node = lane[0:1] // OBJ
    weight = jnp.zeros((1, LANES), F32)
    for m in range(16):
        weight = jnp.where(node == m, float(FACE_W[m]), weight)
    moment = moment * weight
    for shift in (8, 16, 32, 64):
        moment = moment + pltpu.roll(moment, shift, 1)
    moment = moment * jnp.broadcast_to(stats[:, 0:1], (CAP, LANES))
    moment = jnp.where(
        lane < OBJ, moment,
        jnp.where(lane == OBJ, jnp.broadcast_to(stats[:, 1:2], (CAP, LANES)), 0.0),
    )
    spread = lax.broadcasted_iota(jnp.int32, (LANES, 4 * LANES), 0)
    group = lax.broadcasted_iota(jnp.int32, (LANES, 4 * LANES), 1) // CAP
    wide = jnp.dot(
        moment, jnp.where(spread == group, 1.0, 0.0), precision=HIGHEST,
        preferred_element_type=F32,
    )
    slot = lax.broadcasted_iota(jnp.int32, (CAP, 4 * LANES), 0)
    within = lax.broadcasted_iota(jnp.int32, (CAP, 4 * LANES), 1) % CAP
    flat = jnp.sum(jnp.where(slot == within, wide, 0.0), axis=0, keepdims=True)
    square[0:8, :] = jnp.zeros((8, LANES), F32)
    square[0:1, 0:CAP] = ids_ref[...].astype(F32)
    square[1:3, 0:OBJ] = res_ref[...]
    head = square[0:8, :]
    extra = (
        pltpu.roll(head, 32, 1)[0:1] + pltpu.roll(head, 64, 1)[1:2] + pltpu.roll(head, 72, 1)[2:3]
    )
    message = jnp.concatenate(
        [
            flat[:, 0:LANES],
            flat[:, LANES : 2 * LANES],
            flat[:, 2 * LANES : 3 * LANES] + extra,
            jnp.zeros((1, LANES), F32),
        ],
        axis=0,
    )
    double = jnp.concatenate([message, message], axis=0)
    for peer in range(64):
        message_ref[peer * 8 : (peer + 1) * 8, :] = double


def line_nodes(direction, line):
    p, q = line // 4, line % 4
    if direction == 0:
        return [16 * i + 4 * p + q for i in range(4)]
    if direction == 1:
        return [16 * p + 4 * i + q for i in range(4)]
    return [16 * p + 4 * q + i for i in range(4)]


def even_odd(v):
    return v[0] + v[3], v[1] + v[2], v[0] - v[3], v[1] - v[2]


STIFF = DERIV.T @ DERIV
EP, EQ = [0.5 * (DERIV[r, 0] - DERIV[3 - r, 0]) for r in range(2)]
OS = [0.5 * (DERIV[0, i] + DERIV[3, i]) for i in range(2)]
OT = [0.5 * (DERIV[1, i] + DERIV[2, i]) for i in range(2)]
KE = 0.5 * (STIFF[0, 0] + STIFF[0, 3])
KP = [0.5 * (STIFF[i, 0] - STIFF[i, 3]) for i in range(2)]
KQ = [0.5 * (STIFF[i, 1] - STIFF[i, 2]) for i in range(2)]


def transposed_parts(y):
    s, t, p, q = even_odd(y)
    even = float(EP) * p + float(EQ) * q
    odd = [float(OS[i]) * s + float(OT[i]) * t for i in range(2)]
    return even, odd


def combine(even, odd):
    return [odd[0] + even, odd[1] - even, -even - odd[1], even - odd[0]]


def acc_rows(comp, node, half):
    return pl.ds(((half * COMPS + comp) * NODES + node) * 8, 8)


def spread_row(ref, row):
    return ref[pl.ds(row, 8, stride=0), :]


def resolve_outlets(ids_ref, messages_ref, square, gathered, mult_ref, outlet_ref):
    rank = lax.axis_index("dom").astype(jnp.int32)
    for q in range(3):
        rows = messages_ref[pl.ds(q, LANES, stride=MSG), :]
        gathered[q * LANES : (q + 1) * LANES, :] = jnp.transpose(rows)
    square[...] = jnp.zeros((LANES, LANES), F32)
    square[0:1, 0:CAP] = ids_ref[...].astype(F32)
    own_ids = jnp.transpose(square[...])[0:CAP, 0:1]
    sub = lax.broadcasted_iota(jnp.int32, (8, LANES), 0)
    wanted = jnp.concatenate(
        [(rank * 8 + sub).astype(F32), jnp.broadcast_to(own_ids, (CAP, LANES))], axis=0
    )

    def step(t, sums):
        hit = [
            wanted[g * 8 : g * 8 + 8] == spread_row(gathered, 2 * LANES + CAP + t)
            for g in range(5)
        ]
        new = []
        for r in range(9):
            row = spread_row(gathered, r * CAP + t)
            for g in range(5):
                new.append(sums[r * 5 + g] + jnp.where(hit[g], row, 0.0))
        return tuple(new)

    sums = lax.fori_loop(
        0, CAP, step, tuple(jnp.zeros((8, LANES), F32) for _ in range(45))
    )
    device = lax.broadcasted_iota(jnp.int32, (8, LANES), 1).astype(F32)
    for g in range(5):
        linear = jnp.zeros((8, LANES), F32)
        quadratic = jnp.zeros((8, LANES), F32)
        for q in range(8):
            hit = wanted[g * 8 : g * 8 + 8] == device * 8.0 + float(q)
            linear += jnp.where(hit, spread_row(gathered, 2 * LANES + 64 + q), 0.0)
            quadratic += jnp.where(hit, spread_row(gathered, 2 * LANES + 72 + q), 0.0)
        flow = jnp.sum(sums[8 * 5 + g], axis=1, keepdims=True)
        factor = jnp.sum(linear, axis=1, keepdims=True) + 2.0 * jnp.sum(
            quadratic, axis=1, keepdims=True
        ) * jnp.abs(flow)
        lane = lax.broadcasted_iota(jnp.int32, (8, LANES), 1)
        table = jnp.zeros((8, LANES), F32)
        for o in range(OBJ):
            adj = jnp.sum(sums[o * 5 + g], axis=1, keepdims=True)
            table = jnp.where(lane == o, factor * adj, table)
        if g == 0:
            square[...] = jnp.zeros((LANES, LANES), F32)
            square[0:8, :] = table
            mult_ref[...] = jnp.transpose(square[...])[0:8, 0:8]
        else:
            outlet_ref[(g - 1) * 8 : g * 8, :] = table


def gather_pairs(work, partner_ref, pairs_ref, targets_ref, traces, pick):
    partner = partner_ref[...].astype(F32)
    ids = (
        lax.broadcasted_iota(jnp.int32, (6, ELEMS), 1)
        + lax.broadcasted_iota(jnp.int32, (6, ELEMS), 0) * ELEMS
    ).astype(F32)
    first = partner > ids
    flags = jnp.where(first, 1.0, 0.0)
    before = jnp.where(
        lax.broadcasted_iota(jnp.int32, (ELEMS, ELEMS), 0)
        < lax.broadcasted_iota(jnp.int32, (ELEMS, ELEMS), 1),
        1.0, 0.0,
    ).astype(BF16)
    padded = jnp.concatenate([flags, jnp.zeros((10, ELEMS), F32)], axis=0).astype(BF16)
    inside = jnp.dot(padded, before, preferred_element_type=F32)
    number = lax.broadcasted_iota(jnp.int32, (256, LANES), 0).astype(F32)
    offset = jnp.zeros((1, 1), F32)
    ranks = []
    for face in range(6):
        ranks.append(
            jnp.where(first[face : face + 1], inside[face : face + 1] + offset, -1.0)
        )
        offset = offset + jnp.sum(flags[face : face + 1], axis=1, keepdims=True)
    for which, table in enumerate((ids, partner)):
        found = jnp.zeros((256, LANES), F32)
        for face in range(6):
            for half in range(2):
                cut = lane_slice(half)
                found += jnp.where(
                    number == ranks[face][:, cut], table[face : face + 1, cut], 0.0
                )
        column = jnp.sum(found, axis=1, keepdims=True)
        targets_ref[256 * (1 - which) : 256 * (2 - which), :] = jnp.broadcast_to(
            column, (256, LANES)
        )
    row = jnp.concatenate(
        [
            jnp.transpose(targets_ref[start : start + LANES, :])[0:1]
            for start in (256, 384, 0, 128)
        ],
        axis=1,
    )
    fill_pick(pick, row)
    for comp in range(COMPS):
        fill_traces(work, traces, comp)
    pairs_ref[...] = jnp.dot(
        traces[...], pick[...], preferred_element_type=F32
    ).astype(BF16)


def start_copies(pairs, sems):
    copies = [
        pltpu.make_async_copy(src, dst, sems.at[i]) for i, (src, dst) in enumerate(pairs)
    ]
    for copy in copies:
        copy.start()
    return copies


def place_outer(pairs_ref, targets_ref, link_ref, outlet_ref, shared, slots, square, lhs, chosen, outer):
    columns = slot_columns(link_ref, outlet_ref, square)
    slots[LEVELS * CAP :, :] = jnp.zeros((CAP, 4 * LANES), F32)
    for level in range(LEVELS):
        for comp in range(COMPS):
            slots[level * CAP : (level + 1) * CAP, lane_slice(comp)] = shared[level][
                comp * CAP : (comp + 1) * CAP, :
            ]
    lhs[:, 0:512] = pairs_ref[...]
    for comp in range(COMPS):
        high, low = split2(jnp.transpose(slots[:, lane_slice(comp)]))
        lhs[lane_slice(comp), 512:] = high
        lhs[512 + comp * LANES : 512 + (comp + 1) * LANES, 512:] = low
    for face in range(6):
        chosen[0:512, :] = one_hot(targets_ref[...], face)
        chosen[512:, :] = one_hot(columns, face)
        both = jnp.dot(lhs[...], chosen[...], preferred_element_type=F32)
        outer[face * 512 : (face + 1) * 512, :] = both[:512] + both[512:]


def main_kernel(
    x_any, vel_any, metric_any, scale_any, deriv_any, partner_any, link_any, outlet_any,
    s0_ref, s1_ref, s2_ref, s3_ref, s4_ref, s5_ref, s6_ref,
    acc_any,
    x_ref, vel_ref, metric_ref, scale_ref, deriv_ref, partner_ref, link_ref, outlet_ref,
    acc_ref, pairs_ref, targets_ref, work, flux, plain, grads, traces, pick,
    slots, square, lhs, chosen, outer, sems, sem_out,
):
    blocks = [
        (x_any.at[pl.ds(c * 1024, 1024), :], x_ref.at[pl.ds(c * 1024, 1024), :])
        for c in range(COMPS)
    ]
    small = [
        (vel_any, vel_ref), (metric_any, metric_ref), (scale_any, scale_ref),
        (deriv_any, deriv_ref), (partner_any, partner_ref), (link_any, link_ref),
        (outlet_any, outlet_ref),
    ]
    shared = (s0_ref, s1_ref, s2_ref, s3_ref, s4_ref, s5_ref, s6_ref)
    copies = start_copies(small + blocks, sems)
    for copy in copies[:7]:
        copy.wait()
    for comp in range(COMPS):
        copies[7 + comp].wait()
        node_major(x_ref, work, comp)
    gather_pairs(work, partner_ref, pairs_ref, targets_ref, traces, pick)
    place_outer(
        pairs_ref, targets_ref, link_ref, outlet_ref, shared, slots, square, lhs, chosen, outer
    )
    for j in range(3):
        product = jnp.dot(deriv_ref[...], vel_ref[j], preferred_element_type=F32)
        product = (product[0:192] + product[192:384]) + product[384:576]
        velocity = vel_ref[j].astype(F32)
        for half in range(2):
            cut = lane_slice(half)
            row = (j * 2 + half) * NODES
            plain[row : row + NODES, :] = velocity[:, cut]
            flux[row : row + NODES, :] = velocity[:, cut] * metric_ref[j : j + 1, cut]
            for c in range(3):
                row = ((c * 3 + j) * 2 + half) * NODES
                grads[row : row + NODES, :] = (
                    product[c * NODES : (c + 1) * NODES, cut] * metric_ref[c : c + 1, cut]
                )
    stores = []
    for half in range(2):
        cut = lane_slice(half)
        for direction in range(3):
            gain = jnp.broadcast_to(metric_ref[direction : direction + 1, cut], (8, LANES))
            visc = float(VISCOUS) * gain * gain
            v_even = visc * float(KE)
            v_p = [visc * float(KP[i]) for i in range(2)]
            v_q = [visc * float(KQ[i]) for i in range(2)]
            for line in range(16):
                nodes = line_nodes(direction, line)
                values = []
                for comp in range(COMPS):
                    values.append([work[acc_rows(comp, n, half), :] for n in nodes])
                inner = [None] * 4
                gains = [[]] * 4
                if direction == 2:
                    inner = [inner_gain(plain, scale_ref, n, half) for n in nodes]
                    gains = [
                        [
                            (face, m, node_gain(plain, scale_ref, face, n, half))
                            for face, m in touching(n)
                        ]
                        for n in nodes
                    ]
                base = (direction * 2 + half) * NODES
                speed = [spread_row(flux, base + n) for n in nodes]
                for comp in range(COMPS):
                    if comp < 3:
                        y = [speed[i] * values[comp][i] for i in range(4)]
                        if comp == direction:
                            y = [y[i] + gain * values[3][i] for i in range(4)]
                        even, odd = transposed_parts(y)
                        s, t, p, q = even_odd(values[comp])
                        even = even + v_even * (s - t)
                        odd = [odd[i] + (v_p[i] * p + v_q[i] * q) for i in range(2)]
                    else:
                        even, odd = transposed_parts(values[direction])
                        even = gain * even
                        odd = [gain * odd[i] for i in range(2)]
                    out = combine(even, odd)
                    for i, n in enumerate(nodes):
                        result = out[i]
                        if direction > 0:
                            result = result + acc_ref[acc_rows(comp, n, half), :]
                        if direction == 2 and comp < 3:
                            for j in range(3):
                                row = ((comp * 3 + j) * 2 + half) * NODES + n
                                result = result + spread_row(grads, row) * values[j][i]
                        if inner[i] is not None:
                            result = result + inner[i] * values[comp][i]
                        for face, m, face_gain in gains[i]:
                            row = face * 512 + (comp * 16 + m) * OBJ
                            result = result - face_gain * outer[row : row + 8, cut]
                        acc_ref[acc_rows(comp, n, half), :] = result
        part = pl.ds(half * 2048, 2048)
        store = pltpu.make_async_copy(acc_ref.at[part, :], acc_any.at[part, :], sem_out.at[half])
        store.start()
        stores.append(store)
    for store in stores:
        store.wait()


def inner_gain(plain, scale_ref, node, half):
    total = None
    for face, _ in touching(node):
        speed = spread_row(plain, ((face // 2) * 2 + half) * NODES + node)
        part = jnp.maximum(-speed if face % 2 else speed, 0.0) + float(PENALTY)
        part = part * jnp.broadcast_to(scale_ref[face : face + 1, lane_slice(half)], (8, LANES))
        total = part if total is None else total + part
    return total


def outer_gain(vel_row, scale_row, face):
    signed = vel_row if face % 2 else -vel_row
    return scale_row * (jnp.maximum(signed, 0.0) + float(PENALTY))


def touching(node):
    digits = [node // 16, (node // 4) % 4, node % 4]
    found = []
    for d in range(3):
        if digits[d] in (0, 3):
            rest = digits[:d] + digits[d + 1 :]
            found.append((2 * d + digits[d] // 3, 4 * rest[0] + rest[1]))
    return found


def node_gain(plain, scale_ref, face, node, half):
    scale = jnp.broadcast_to(scale_ref[face : face + 1, lane_slice(half)], (8, LANES))
    return outer_gain(spread_row(plain, ((face // 2) * 2 + half) * NODES + node), scale, face)


def final_kernel(
    live_any, acc_any, scale_any, link_any, outlet_any, ids_any, messages_ref,
    out_any, mult_ref,
    live_ref, acc_ref, scale_ref, link_ref, outlet_ref, ids_ref,
    out_ref, square, outlet, gathered, terms, sems, sem_out,
):
    copies = start_copies(
        [
            (ids_any, ids_ref), (link_any, link_ref),
            (outlet_any, outlet_ref), (scale_any, scale_ref), (live_any, live_ref),
            (acc_any, acc_ref),
        ],
        sems,
    )
    for copy in copies[:5]:
        copy.wait()
    resolve_outlets(ids_ref, messages_ref, square, gathered, mult_ref, terms)
    columns = slot_columns(link_ref, outlet_ref, square)[LEVELS * CAP :]
    square[...] = jnp.zeros((LANES, LANES), F32)
    square[0:CAP, :] = terms[...]
    high, low = split2(jnp.transpose(square[...])[0:16, 0:CAP])
    both = jnp.concatenate([high, low], axis=0)
    for face in range(6):
        term = jnp.dot(both, one_hot(columns, face), preferred_element_type=F32)
        scale = scale_ref[face : face + 1, :] * (2.0 * (face % 2) - 1.0)
        outlet[face * 8 : (face + 1) * 8, :] = (term[0:8] + term[16:24]) * scale
    copies[5].wait()
    live = [live_ref[:, lane_slice(half)] > 0.5 for half in range(2)]
    stores = []
    for high in range(8):
        for half in range(2):
            cut = lane_slice(half)
            block = [[] for _ in range(COMPS)]
            for n in range(high * 8, high * 8 + 8):
                results = [acc_ref[acc_rows(comp, n, half), :] for comp in range(COMPS)]
                for face, m in touching(n):
                    axis = face // 2
                    results[axis] = (
                        results[axis] + float(FACE_W[m]) * outlet[face * 8 : face * 8 + 8, cut]
                    )
                for comp in range(COMPS):
                    block[comp].append(jnp.where(live[half], results[comp], 0.0))
            for comp in range(COMPS):
                turned_block = jnp.swapaxes(jnp.stack(block[comp]), 0, 1)
                out_ref[comp * OBJ : (comp + 1) * OBJ, high, half * 8 : half * 8 + 8, :] = (
                    turned_block
                )
        store = pltpu.make_async_copy(
            out_ref.at[:, high], out_any.at[:, high], sem_out.at[high]
        )
        store.start()
        stores.append(store)
    for store in stores:
        store.wait()


VMEM = pl.BlockSpec(memory_space=pltpu.VMEM)
ANY = pl.BlockSpec(memory_space=pltpu.MemorySpace.HBM)


def params(mebibytes):
    return pltpu.CompilerParams(vmem_limit_bytes=mebibytes * 2**20)


def cost(microseconds):
    return pl.CostEstimate(
        flops=int(microseconds * 1e3), bytes_accessed=int(microseconds * 3.0e6), transcendentals=0
    )


def f32(*shape):
    return jax.ShapeDtypeStruct(shape, F32)


def local(
    adjoint, velocity, metric, face_scale, resistance, elem_count, face_partner, link_face,
    outlet_face, outlet_id,
):
    x_view = (
        adjoint.reshape(COMPS, OBJ, 8, 8, 2, LANES).transpose(0, 1, 2, 4, 3, 5).reshape(4096, LANES)
    )
    link = link_face.transpose(1, 0, 2)
    deriv = jnp.asarray(np.concatenate(split3(node_matrices())), BF16)
    flow = jnp.asarray(flow_matrix(), BF16)
    devices = lax.axis_size("dom")

    message, live, *sent = pl.pallas_call(
        gather_kernel,
        out_shape=(f32(devices * MSG, LANES), f32(8, ELEMS))
        + (f32(FACE_ROWS, LANES),) * LEVELS,
        in_specs=[ANY] * 9,
        out_specs=(VMEM,) * (2 + LEVELS),
        scratch_shapes=[
            pltpu.VMEM((4096, LANES), F32), pltpu.VMEM((3, NODES, ELEMS), BF16),
            pltpu.VMEM((6, ELEMS), F32), pltpu.VMEM((LEVELS, 1, CAP), jnp.int32),
            pltpu.VMEM((1, CAP), jnp.int32), pltpu.VMEM((1, CAP), jnp.int32),
            pltpu.VMEM((2, OBJ), F32), pltpu.VMEM((48, NODES), BF16),
            pltpu.VMEM((1, 1), jnp.int32), pltpu.VMEM((4096, LANES), F32),
            pltpu.VMEM((1040, 6 * ELEMS), BF16), pltpu.VMEM((6 * ELEMS, 256), BF16),
            pltpu.VMEM((LANES, LANES), F32), pltpu.VMEM((256, 512), F32),
            pltpu.SemaphoreType.DMA((12,)),
        ],
        compiler_params=params(60),
        cost_estimate=cost(5),
        name="gather",
    )(x_view, velocity, face_scale, link, outlet_face, outlet_id, resistance, flow,
      elem_count.reshape(1, 1))

    messages = lax.all_to_all(
        message.reshape(devices, MSG, LANES), "dom", split_axis=0, concat_axis=0, tiled=True
    ).reshape(devices * MSG, LANES)

    def swap(block, mask):
        return lax.ppermute(block, "dom", [(i, i ^ mask) for i in range(devices)])

    received = []
    for level, block in enumerate(sent):
        received.append(swap(block, 1 << level))
    acc = pl.pallas_call(
        main_kernel,
        out_shape=f32(4096, LANES),
        in_specs=[ANY] * 8 + [VMEM] * LEVELS,
        out_specs=ANY,
        scratch_shapes=[
            pltpu.VMEM((4096, LANES), F32), pltpu.VMEM((3, NODES, ELEMS), BF16),
            pltpu.VMEM((3, ELEMS), F32), pltpu.VMEM((6, ELEMS), F32),
            pltpu.VMEM((576, NODES), BF16), pltpu.VMEM((6, ELEMS), jnp.int32),
            pltpu.VMEM((LEVELS, 1, CAP), jnp.int32), pltpu.VMEM((1, CAP), jnp.int32),
            pltpu.VMEM((4096, LANES), F32), pltpu.VMEM((1024, 512), BF16),
            pltpu.VMEM((512, LANES), F32), pltpu.VMEM((4096, LANES), F32),
            pltpu.VMEM((384, LANES), F32), pltpu.VMEM((384, LANES), F32),
            pltpu.VMEM((1152, LANES), F32), pltpu.VMEM((1024, 6 * ELEMS), BF16),
            pltpu.VMEM((6 * ELEMS, 512), BF16), pltpu.VMEM((256, 512), F32),
            pltpu.VMEM((LANES, LANES), F32), pltpu.VMEM((1024, 768), BF16),
            pltpu.VMEM((768, ELEMS), BF16), pltpu.VMEM((6 * 512, ELEMS), F32),
            pltpu.SemaphoreType.DMA((11,)), pltpu.SemaphoreType.DMA((2,)),
        ],
        compiler_params=params(30),
        cost_estimate=cost(10),
        name="volume",
    )(
        x_view, velocity, metric, face_scale, deriv, face_partner, link, outlet_face, *received
    )

    out, multiplier = pl.pallas_call(
        final_kernel,
        out_shape=(f32(32, 8, 16, LANES), f32(OBJ, 8)),
        in_specs=[ANY] * 6 + [VMEM],
        out_specs=(ANY, VMEM),
        scratch_shapes=[
            pltpu.VMEM((8, ELEMS), F32), pltpu.VMEM((4096, LANES), F32),
            pltpu.VMEM((6, ELEMS), F32), pltpu.VMEM((LEVELS, 1, CAP), jnp.int32),
            pltpu.VMEM((1, CAP), jnp.int32), pltpu.VMEM((1, CAP), jnp.int32),
            pltpu.VMEM((32, 8, 16, LANES), F32),
            pltpu.VMEM((LANES, LANES), F32), pltpu.VMEM((48, ELEMS), F32),
            pltpu.VMEM((384, LANES), F32), pltpu.VMEM((CAP, LANES), F32),
            pltpu.SemaphoreType.DMA((6,)), pltpu.SemaphoreType.DMA((8,)),
        ],
        compiler_params=params(30),
        cost_estimate=cost(3),
        name="finish",
    )(live, acc, face_scale, link, outlet_face, outlet_id, messages)
    out = (
        out.reshape(COMPS, OBJ, 8, 2, 8, LANES).transpose(0, 1, 2, 4, 3, 5)
        .reshape(COMPS, OBJ, NODES, ELEMS)
    )
    return out, multiplier


def solution(mesh):
    placed = (
        P(None, None, None, "dom"), P(None, None, "dom"), P(None, "dom"), P(None, "dom"),
        P(None, "dom"), P("dom"), P(None, "dom"), P("dom", None, None), P("dom", None),
        P("dom", None),
    )
    return jax.shard_map(
        local, mesh=mesh, in_specs=placed,
        out_specs=(P(None, None, None, "dom"), P(None, "dom")), check_vma=False,
    )
```

profile of v0, /device:TPU:0, one launch (start us, length us, event | category | flops | bytes accessed | tf_op | source)
XLA Modules:
  0.0 49.5 jit_solution(11394261301451332286)
XLA Ops:
  0.6 0.0 copy-start.4
  0.6 0.0 copy-start.9
  0.7 0.0 copy-start.5
  0.7 0.0 copy-start.3
  0.7 0.0 copy-start.6
  0.7 0.0 copy-start
  0.7 0.0 copy-start.7
  0.7 0.0 copy-start.10
  1.5 5.0 %gather.1 = (f32[512,128]{1,0:T(8,128)}, f32[8,256]{1,0:T(8,128)}, f32[128,128]{1,0:T(8,128)}, f32[128,128]{1,0:T(8,128)}, f32[128,128]{1,0:T(8,128)}, /*index=5...) custom-call(f32[4096,128]{1,0:T(8,128)} %bitcast.15, bf16[3,64,256]{2,1,0:T(8,128)(2,1)} %vel_any.3, ...), custom_call_target="tpu_custom_call" | custom-call | flops 5000 | bytes 15000000 | tf_op jit(solution)/shard_map/gather/pallas_call | solution.py:682
  6.6 11.2 %all-to-all-start = ((f32[128,4,128]{2,1,0:T(4,128)}), f32[128,4,128]{2,1,0:T(4,128)S(1)}, u32[]{:S(2)}, u32[]{:S(2)}) async-start(f32[128,4,128]{2,1,0:T(4,128)} %bitcast.21), calls=%async_computation | async-start | bytes 524288 | tf_op jit(solution)/shard_map/all_to_all | solution.py:704
  17.7 0.1 collective-permute-start
  17.8 1.2 %collective-permute-start.1 = (f32[128,128]{1,0:T(8,128)}, f32[128,128]{1,0:T(8,128)S(1)}, u32[]{:S(2)}, u32[]{:S(2)}) collective-permute-start(f32[128,128]{1,0:T(8,128)} %get-tuple-element.15), channel_id=1, source_target_pairs={{0,2},{1,3},{2,0},{3,1},{4,6},{5,7},{6,4},{7,5},{8,10},{9,11},{10,... | collective-permute-start | bytes 196616 | tf_op jit(solution)/shard_map/ppermute | solution.py:709
  19.0 3.2 %collective-permute-start.2 = (f32[128,128]{1,0:T(8,128)}, f32[128,128]{1,0:T(8,128)S(1)}, u32[]{:S(2)}, u32[]{:S(2)}) collective-permute-start(f32[128,128]{1,0:T(8,128)} %get-tuple-element.16), channel_id=1, source_target_pairs={{0,4},{1,5},{2,6},{3,7},{4,0},{5,1},{6,2},{7,3},{8,12},{9,13},{10,... | collective-permute-start | bytes 196616 | tf_op jit(solution)/shard_map/ppermute | solution.py:709
  22.2 1.5 %collective-permute-start.3 = (f32[128,128]{1,0:T(8,128)}, f32[128,128]{1,0:T(8,128)S(1)}, u32[]{:S(2)}, u32[]{:S(2)}) collective-permute-start(f32[128,128]{1,0:T(8,128)} %get-tuple-element.17), channel_id=1, source_target_pairs={{0,8},{1,9},{2,10},{3,11},{4,12},{5,13},{6,14},{7,15},{8,0},{9,1},... | collective-permute-start | bytes 196616 | tf_op jit(solution)/shard_map/ppermute | solution.py:709
  23.8 2.8 %collective-permute-start.4 = (f32[128,128]{1,0:T(8,128)}, f32[128,128]{1,0:T(8,128)S(1)}, u32[]{:S(2)}, u32[]{:S(2)}) collective-permute-start(f32[128,128]{1,0:T(8,128)} %get-tuple-element.18), channel_id=1, source_target_pairs={{0,16},{1,17},{2,18},{3,19},{4,20},{5,21},{6,22},{7,23},{8,24},{9,... | collective-permute-start | bytes 196616 | tf_op jit(solution)/shard_map/ppermute | solution.py:709
  26.6 0.0 collective-permute-done.s0_ref
  26.6 1.5 %collective-permute-start.5 = (f32[128,128]{1,0:T(8,128)}, f32[128,128]{1,0:T(8,128)S(1)}, u32[]{:S(2)}, u32[]{:S(2)}) collective-permute-start(f32[128,128]{1,0:T(8,128)} %get-tuple-element.19), channel_id=1, source_target_pairs={{0,32},{1,33},{2,34},{3,35},{4,36},{5,37},{6,38},{7,39},{8,40},{9,... | collective-permute-start | bytes 196616 | tf_op jit(solution)/shard_map/ppermute | solution.py:709
  28.1 0.0 collective-permute-done.1.s1_ref
  28.1 0.0 copy-start.8
  28.1 0.0 copy-start.11
  28.1 2.7 %collective-permute-start.6 = (f32[128,128]{1,0:T(8,128)}, f32[128,128]{1,0:T(8,128)S(1)}, u32[]{:S(2)}, u32[]{:S(2)}) collective-permute-start(f32[128,128]{1,0:T(8,128)} %get-tuple-element.20), channel_id=1, source_target_pairs={{0,64},{1,65},{2,66},{3,67},{4,68},{5,69},{6,70},{7,71},{8,72},{9,... | collective-permute-start | bytes 196616 | tf_op jit(solution)/shard_map/ppermute | solution.py:709
  30.8 0.0 collective-permute-done.2.s2_ref
  30.8 0.0 collective-permute-done.3.s3_ref
  30.8 0.0 collective-permute-done.4.s4_ref
  30.8 0.4 collective-permute-done.5.s5_ref
  31.2 2.8 %collective-permute-done.6.s6_ref = f32[128,128]{1,0:T(8,128)S(1)} collective-permute-done((f32[128,128]{1,0:T(8,128)}, f32[128,128]{1,0:T(8,128)S(1)}, u32[]{:S(2)}, u32[]{:S(2)}) %collective-permute-start.6) | collective-permute-done | bytes 65568 | tf_op jit(solution)/shard_map/ppermute | solution.py:709
  34.1 0.0 copy-done.4
  34.1 0.0 copy-done.9
  34.1 0.0 copy-done.5
  34.1 0.0 copy-done.3
  34.1 0.0 copy-done.6
  34.1 0.0 copy-done
  34.1 0.0 copy-done.7
  34.1 0.0 copy-done.10
  34.1 8.6 %volume.1.acc_any = f32[4096,128]{1,0:T(8,128)S(1)} custom-call(f32[4096,128]{1,0:T(8,128)S(1)} %bitcast.16, bf16[3,64,256]{2,1,0:T(8,128)(2,1)S(1)} %copy-done.3, f32[3,256]{1,0:T(4,128)S(1)} %copy-done.10, f32[6,256]{1,0:T(8,128)S(1)} %copy-done.5, bf16[576,64]{1,0:T(8,128)(2,1)S(1)} %copy-done.4, s32[6,256]{1,0:T(8,128)S(1)} %copy-done.7, ...), custom_call_target="tpu_custom_call" | custom-call | flops 10000 | bytes 30000000 | tf_op jit(solution)/shard_map/volume/pallas_call | solution.py:714
  42.7 0.0 copy-start.1
  42.7 1.3 %copy-done.1 = f32[4096,128]{1,0:T(8,128)} copy-done((f32[4096,128]{1,0:T(8,128)}, f32[4096,128]{1,0:T(8,128)S(1)}, u32[]{:S(2)}) %copy-start.1) | copy-done | bytes 2097176
  44.0 0.0 all-to-all-done
  44.0 0.0 copy-done.8
  44.0 0.0 copy-done.11
  44.0 0.0 copy-start.2
  44.1 1.6 %copy-done.2 = f32[4096,128]{1,0:T(8,128)S(1)} copy-done((f32[4096,128]{1,0:T(8,128)S(1)}, f32[4096,128]{1,0:T(8,128)}, u32[]{:S(2)}) %copy-start.2) | copy-done | bytes 2097176
  45.6 3.7 %finish.1 = (f32[32,8,16,128]{3,2,1,0:T(8,128)}, f32[8,8]{1,0:T(8,128)}) custom-call(f32[8,256]{1,0:T(8,128)S(1)} %copy-done.8, f32[4096,128]{1,0:T(8,128)S(1)} %copy-done.2, f32[6,256]{1,0:T(8,128)S(1)} %copy-done.5, s32[7,1,32]{2,1,0:T(1,128)S(1)} %bitcast.20, s32[1,32]{1,0:T(1,128)S(1)} %copy-done.9, s32[1,32]{1,0:T(1,128)S(1)} %copy-done.11, ...), custom_call_target="tpu_custom_call" | custom-call | flops 3000 | bytes 9000000 | tf_op jit(solution)/shard_map/finish/pallas_call | solution.py:740
Async XLA Ops:
  0.6 33.4 %copy-start.4 = (bf16[576,64]{1,0:T(8,128)(2,1)S(1)}, bf16[576,64]{1,0:T(8,128)(2,1)}, u32[]{:S(2)}) copy-start(bf16[576,64]{1,0:T(8,128)(2,1)} %constant.4.clone.deriv_any) | copy-start | bytes 221188
  0.6 33.4 %copy-start.9 = (s32[1,32]{1,0:T(1,128)S(1)}, s32[1,32]{1,0:T(1,128)}, u32[]{:S(2)}) copy-start(s32[1,32]{1,0:T(1,128)} %outlet_any.5) | copy-start | bytes 388
  0.7 33.4 %copy-start.5 = (f32[6,256]{1,0:T(8,128)S(1)}, f32[6,256]{1,0:T(8,128)}, u32[]{:S(2)}) copy-start(f32[6,256]{1,0:T(8,128)} %scale_any.5) | copy-start | bytes 18436
  0.7 33.4 %copy-start.3 = (bf16[3,64,256]{2,1,0:T(8,128)(2,1)S(1)}, bf16[3,64,256]{2,1,0:T(8,128)(2,1)}, u32[]{:S(2)}) copy-start(bf16[3,64,256]{2,1,0:T(8,128)(2,1)} %vel_any.3) | copy-start | bytes 294916
  0.7 33.4 %copy-start.6 = (s32[1,7,32]{2,0,1:T(1,128)S(1)}, s32[1,7,32]{2,0,1:T(1,128)}, u32[]{:S(2)}) copy-start(s32[1,7,32]{2,0,1:T(1,128)} %param.19) | copy-start | bytes 2692
  0.7 33.4 %copy-start = (f32[4,8,64,256]{3,2,1,0:T(8,128)S(1)}, f32[4,8,64,256]{3,2,1,0:T(8,128)}, u32[]{:S(2)}) copy-start(f32[4,8,64,256]{3,2,1,0:T(8,128)} %param.12) | copy-start | bytes 6291460
  0.7 33.4 %copy-start.7 = (s32[6,256]{1,0:T(8,128)S(1)}, s32[6,256]{1,0:T(8,128)}, u32[]{:S(2)}) copy-start(s32[6,256]{1,0:T(8,128)} %partner_any.1) | copy-start | bytes 18436
  0.7 33.4 %copy-start.10 = (f32[3,256]{1,0:T(4,128)S(1)}, f32[3,256]{1,0:T(4,128)}, u32[]{:S(2)}) copy-start(f32[3,256]{1,0:T(4,128)} %metric_any.1) | copy-start | bytes 9220
  6.6 37.5 %all-to-all-start = ((f32[128,4,128]{2,1,0:T(4,128)}), f32[128,4,128]{2,1,0:T(4,128)S(1)}, u32[]{:S(2)}, u32[]{:S(2)}) async-start(f32[128,4,128]{2,1,0:T(4,128)} %bitcast.21), calls=%async_computation | async-start | bytes 524288 | tf_op jit(solution)/shard_map/all_to_all | solution.py:704
  17.7 8.8 %collective-permute-start = (f32[128,128]{1,0:T(8,128)}, f32[128,128]{1,0:T(8,128)S(1)}, u32[]{:S(2)}, u32[]{:S(2)}) collective-permute-start(f32[128,128]{1,0:T(8,128)} %get-tuple-element.14), channel_id=1, source_target_pairs={{0,1},{1,0},{2,3},{3,2},{4,5},{5,4},{6,7},{7,6},{8,9},{9,8},{10,11... | collective-permute-start | bytes 196616 | tf_op jit(solution)/shard_map/ppermute | solution.py:709
  17.8 10.2 %collective-permute-start.1 = (f32[128,128]{1,0:T(8,128)}, f32[128,128]{1,0:T(8,128)S(1)}, u32[]{:S(2)}, u32[]{:S(2)}) collective-permute-start(f32[128,128]{1,0:T(8,128)} %get-tuple-element.15), channel_id=1, source_target_pairs={{0,2},{1,3},{2,0},{3,1},{4,6},{5,7},{6,4},{7,5},{8,10},{9,11},{10,... | collective-permute-start | bytes 196616 | tf_op jit(solution)/shard_map/ppermute | solution.py:709
  19.0 11.8 %collective-permute-start.2 = (f32[128,128]{1,0:T(8,128)}, f32[128,128]{1,0:T(8,128)S(1)}, u32[]{:S(2)}, u32[]{:S(2)}) collective-permute-start(f32[128,128]{1,0:T(8,128)} %get-tuple-element.16), channel_id=1, source_target_pairs={{0,4},{1,5},{2,6},{3,7},{4,0},{5,1},{6,2},{7,3},{8,12},{9,13},{10,... | collective-permute-start | bytes 196616 | tf_op jit(solution)/shard_map/ppermute | solution.py:709
  22.2 8.5 %collective-permute-start.3 = (f32[128,128]{1,0:T(8,128)}, f32[128,128]{1,0:T(8,128)S(1)}, u32[]{:S(2)}, u32[]{:S(2)}) collective-permute-start(f32[128,128]{1,0:T(8,128)} %get-tuple-element.17), channel_id=1, source_target_pairs={{0,8},{1,9},{2,10},{3,11},{4,12},{5,13},{6,14},{7,15},{8,0},{9,1},... | collective-permute-start | bytes 196616 | tf_op jit(solution)/shard_map/ppermute | solution.py:709
  23.8 7.0 %collective-permute-start.4 = (f32[128,128]{1,0:T(8,128)}, f32[128,128]{1,0:T(8,128)S(1)}, u32[]{:S(2)}, u32[]{:S(2)}) collective-permute-start(f32[128,128]{1,0:T(8,128)} %get-tuple-element.18), channel_id=1, source_target_pairs={{0,16},{1,17},{2,18},{3,19},{4,20},{5,21},{6,22},{7,23},{8,24},{9,... | collective-permute-start | bytes 196616 | tf_op jit(solution)/shard_map/ppermute | solution.py:709
  26.6 4.6 %collective-permute-start.5 = (f32[128,128]{1,0:T(8,128)}, f32[128,128]{1,0:T(8,128)S(1)}, u32[]{:S(2)}, u32[]{:S(2)}) collective-permute-start(f32[128,128]{1,0:T(8,128)} %get-tuple-element.19), channel_id=1, source_target_pairs={{0,32},{1,33},{2,34},{3,35},{4,36},{5,37},{6,38},{7,39},{8,40},{9,... | collective-permute-start | bytes 196616 | tf_op jit(solution)/shard_map/ppermute | solution.py:709
  28.1 16.0 %copy-start.8 = (f32[8,256]{1,0:T(8,128)S(1)}, f32[8,256]{1,0:T(8,128)}, u32[]{:S(2)}) copy-start(f32[8,256]{1,0:T(8,128)} %get-tuple-element.13.live_any) | copy-start | bytes 24580
  28.1 16.0 %copy-start.11 = (s32[1,32]{1,0:T(1,128)S(1)}, s32[1,32]{1,0:T(1,128)}, u32[]{:S(2)}) copy-start(s32[1,32]{1,0:T(1,128)} %ids_any.3) | copy-start | bytes 388
  28.1 6.0 %collective-permute-start.6 = (f32[128,128]{1,0:T(8,128)}, f32[128,128]{1,0:T(8,128)S(1)}, u32[]{:S(2)}, u32[]{:S(2)}) collective-permute-start(f32[128,128]{1,0:T(8,128)} %get-tuple-element.20), channel_id=1, source_target_pairs={{0,64},{1,65},{2,66},{3,67},{4,68},{5,69},{6,70},{7,71},{8,72},{9,... | collective-permute-start | bytes 196616 | tf_op jit(solution)/shard_map/ppermute | solution.py:709
  42.7 1.3 %copy-start.1 = (f32[4096,128]{1,0:T(8,128)}, f32[4096,128]{1,0:T(8,128)S(1)}, u32[]{:S(2)}) copy-start(f32[4096,128]{1,0:T(8,128)S(1)} %volume.1.acc_any) | copy-start | bytes 6291460
  44.0 1.6 %copy-start.2 = (f32[4096,128]{1,0:T(8,128)S(1)}, f32[4096,128]{1,0:T(8,128)}, u32[]{:S(2)}) copy-start(f32[4096,128]{1,0:T(8,128)} %copy-done.1) | copy-start | bytes 6291460
where the time goes:
time: 49.7 us; the launch traced here: 49.5 us
  starting transfers between devices  24.2 us (49%)
  Pallas kernels  17.3 us (35%)
  waiting for transfers between devices  3.28 us (7%)
  local copies, waits for them, and re-layouts  2.94 us (6%)
  between operations  1.76 us (4%)
    ppermute x7, starting transfers between devices, swap(): return lax.ppermute(block, 'dom', [(i, i ^ mask) for i in range(devices)])  13 us
    all_to_all x1, starting transfers between devices, local(): lax.all_to_all(message.reshape(devices, MSG, LANES), 'dom', split_axis=0,...  11.2 us
    pallas_call x1, Pallas kernels, local(): pl.pallas_call(main_kernel, out_shape=f32(4096, LANES), in_specs=[ANY] *...  8.59 us
    pallas_call x1, Pallas kernels, local(): pl.pallas_call(gather_kernel, out_shape=(f32(devices * MSG, LANES), f32(8...  5.04 us
    pallas_call x1, Pallas kernels, local(): pl.pallas_call(final_kernel, out_shape=(f32(32, 8, 16, LANES), f32(OBJ, 8...  3.65 us
    ppermute x7, waiting for transfers between devices, swap(): return lax.ppermute(block, 'dom', [(i, i ^ mask) for i in range(devices)])  3.27 us
    unnamed x24, local copies, waits for them, and re-layouts  2.94 us
  transfers between devices with their start and end apart: 8, of which 2 were waited for; matrix products, arithmetic and copies ran while one was open for 0% of the time, Pallas kernels for 17%

commit v1 on v0

--- a/solution.py
+++ b/solution.py
@@ -160,16 +160,15 @@
 
 
 def gather_kernel(
-    x_any, vel_any, scale_any, link_any, outlet_any, ids_any, res_any, flow_any, count_any,
-    message_ref, live_ref,
+    x_any, vel_any, scale_any, link_any, outlet_any, ids_any, res_any, flow_any,
+    message_ref,
     s0_ref, s1_ref, s2_ref, s3_ref, s4_ref, s5_ref, s6_ref,
-    x_ref, vel_ref, scale_ref, link_ref, outlet_ref, ids_ref, res_ref, flow_ref, count_ref,
+    x_ref, vel_ref, scale_ref, link_ref, outlet_ref, ids_ref, res_ref, flow_ref,
     work_ref, traces, pick, square, total, sems,
 ):
     small = (
         (link_any, link_ref), (outlet_any, outlet_ref), (vel_any, vel_ref),
         (scale_any, scale_ref), (flow_any, flow_ref), (ids_any, ids_ref), (res_any, res_ref),
-        (count_any, count_ref),
     )
     copies = [
         pltpu.make_async_copy(src, dst, sems.at[4 + i]) for i, (src, dst) in enumerate(small)
@@ -184,8 +183,6 @@
         copy.start()
     for copy in copies:
         copy.wait()
-    element = lax.broadcasted_iota(jnp.int32, (8, ELEMS), 1)
-    live_ref[...] = jnp.where(element < count_ref[...], 1.0, 0.0)
     square[0:8, :] = jnp.zeros((8, LANES), F32)
     for level in range(LEVELS):
         square[level : level + 1, 0:CAP] = link_ref[level].astype(F32)
@@ -459,10 +456,10 @@
 
 
 def main_kernel(
-    x_any, vel_any, metric_any, scale_any, deriv_any, partner_any, link_any, outlet_any,
+    x_any, vel_any, metric_any, scale_any, deriv_any, partner_any, link_any, outlet_any, count_any,
     s0_ref, s1_ref, s2_ref, s3_ref, s4_ref, s5_ref, s6_ref,
     acc_any,
-    x_ref, vel_ref, metric_ref, scale_ref, deriv_ref, partner_ref, link_ref, outlet_ref,
+    x_ref, vel_ref, metric_ref, scale_ref, deriv_ref, partner_ref, link_ref, outlet_ref, count_ref,
     acc_ref, pairs_ref, targets_ref, work, flux, plain, grads, traces, pick,
     slots, square, lhs, chosen, outer, sems, sem_out,
 ):
@@ -473,14 +470,14 @@
     small = [
         (vel_any, vel_ref), (metric_any, metric_ref), (scale_any, scale_ref),
         (deriv_any, deriv_ref), (partner_any, partner_ref), (link_any, link_ref),
-        (outlet_any, outlet_ref),
+        (outlet_any, outlet_ref), (count_any, count_ref),
     ]
     shared = (s0_ref, s1_ref, s2_ref, s3_ref, s4_ref, s5_ref, s6_ref)
     copies = start_copies(small + blocks, sems)
-    for copy in copies[:7]:
+    for copy in copies[:8]:
         copy.wait()
     for comp in range(COMPS):
-        copies[7 + comp].wait()
+        copies[8 + comp].wait()
         node_major(x_ref, work, comp)
     gather_pairs(work, partner_ref, pairs_ref, targets_ref, traces, pick)
     place_outer(
@@ -503,6 +500,8 @@
     stores = []
     for half in range(2):
         cut = lane_slice(half)
+        lane = lax.broadcasted_iota(jnp.int32, (8, LANES), 1) + half * LANES
+        live = lane < count_ref[...]
         for direction in range(3):
             gain = jnp.broadcast_to(metric_ref[direction : direction + 1, cut], (8, LANES))
             visc = float(VISCOUS) * gain * gain
@@ -554,6 +553,8 @@
                         for face, m, face_gain in gains[i]:
                             row = face * 512 + (comp * 16 + m) * OBJ
                             result = result - face_gain * outer[row : row + 8, cut]
+                        if direction == 2:
+                            result = jnp.where(live, result, 0.0)
                         acc_ref[acc_rows(comp, n, half), :] = result
         part = pl.ds(half * 2048, 2048)
         store = pltpu.make_async_copy(acc_ref.at[part, :], acc_any.at[part, :], sem_out.at[half])
@@ -594,20 +595,20 @@
 
 
 def final_kernel(
-    live_any, acc_any, scale_any, link_any, outlet_any, ids_any, messages_ref,
+    acc_any, scale_any, link_any, outlet_any, ids_any, messages_ref,
     out_any, mult_ref,
-    live_ref, acc_ref, scale_ref, link_ref, outlet_ref, ids_ref,
+    acc_ref, scale_ref, link_ref, outlet_ref, ids_ref,
     out_ref, square, outlet, gathered, terms, sems, sem_out,
 ):
     copies = start_copies(
         [
             (ids_any, ids_ref), (link_any, link_ref),
-            (outlet_any, outlet_ref), (scale_any, scale_ref), (live_any, live_ref),
+            (outlet_any, outlet_ref), (scale_any, scale_ref),
             (acc_any, acc_ref),
         ],
         sems,
     )
-    for copy in copies[:5]:
+    for copy in copies[:4]:
         copy.wait()
     resolve_outlets(ids_ref, messages_ref, square, gathered, mult_ref, terms)
     columns = slot_columns(link_ref, outlet_ref, square)[LEVELS * CAP :]
@@ -619,8 +620,7 @@
         term = jnp.dot(both, one_hot(columns, face), preferred_element_type=F32)
         scale = scale_ref[face : face + 1, :] * (2.0 * (face % 2) - 1.0)
         outlet[face * 8 : (face + 1) * 8, :] = (term[0:8] + term[16:24]) * scale
-    copies[5].wait()
-    live = [live_ref[:, lane_slice(half)] > 0.5 for half in range(2)]
+    copies[4].wait()
     stores = []
     for high in range(8):
         for half in range(2):
@@ -634,7 +634,7 @@
                         results[axis] + float(FACE_W[m]) * outlet[face * 8 : face * 8 + 8, cut]
                     )
                 for comp in range(COMPS):
-                    block[comp].append(jnp.where(live[half], results[comp], 0.0))
+                    block[comp].append(results[comp])
             for comp in range(COMPS):
                 turned_block = jnp.swapaxes(jnp.stack(block[comp]), 0, 1)
                 out_ref[comp * OBJ : (comp + 1) * OBJ, high, half * 8 : half * 8 + 8, :] = (
@@ -679,18 +679,18 @@
     flow = jnp.asarray(flow_matrix(), BF16)
     devices = lax.axis_size("dom")
 
-    message, live, *sent = pl.pallas_call(
+    message, *sent = pl.pallas_call(
         gather_kernel,
-        out_shape=(f32(devices * MSG, LANES), f32(8, ELEMS))
+        out_shape=(f32(devices * MSG, LANES),)
         + (f32(FACE_ROWS, LANES),) * LEVELS,
-        in_specs=[ANY] * 9,
-        out_specs=(VMEM,) * (2 + LEVELS),
+        in_specs=[ANY] * 8,
+        out_specs=(VMEM,) * (1 + LEVELS),
         scratch_shapes=[
             pltpu.VMEM((4096, LANES), F32), pltpu.VMEM((3, NODES, ELEMS), BF16),
             pltpu.VMEM((6, ELEMS), F32), pltpu.VMEM((LEVELS, 1, CAP), jnp.int32),
             pltpu.VMEM((1, CAP), jnp.int32), pltpu.VMEM((1, CAP), jnp.int32),
             pltpu.VMEM((2, OBJ), F32), pltpu.VMEM((48, NODES), BF16),
-            pltpu.VMEM((1, 1), jnp.int32), pltpu.VMEM((4096, LANES), F32),
+            pltpu.VMEM((4096, LANES), F32),
             pltpu.VMEM((1040, 6 * ELEMS), BF16), pltpu.VMEM((6 * ELEMS, 256), BF16),
             pltpu.VMEM((LANES, LANES), F32), pltpu.VMEM((256, 512), F32),
             pltpu.SemaphoreType.DMA((12,)),
@@ -698,8 +698,7 @@
         compiler_params=params(60),
         cost_estimate=cost(5),
         name="gather",
-    )(x_view, velocity, face_scale, link, outlet_face, outlet_id, resistance, flow,
-      elem_count.reshape(1, 1))
+    )(x_view, velocity, face_scale, link, outlet_face, outlet_id, resistance, flow)
 
     messages = lax.all_to_all(
         message.reshape(devices, MSG, LANES), "dom", split_axis=0, concat_axis=0, tiled=True
@@ -714,13 +713,14 @@
     acc = pl.pallas_call(
         main_kernel,
         out_shape=f32(4096, LANES),
-        in_specs=[ANY] * 8 + [VMEM] * LEVELS,
+        in_specs=[ANY] * 9 + [VMEM] * LEVELS,
         out_specs=ANY,
         scratch_shapes=[
             pltpu.VMEM((4096, LANES), F32), pltpu.VMEM((3, NODES, ELEMS), BF16),
             pltpu.VMEM((3, ELEMS), F32), pltpu.VMEM((6, ELEMS), F32),
             pltpu.VMEM((576, NODES), BF16), pltpu.VMEM((6, ELEMS), jnp.int32),
             pltpu.VMEM((LEVELS, 1, CAP), jnp.int32), pltpu.VMEM((1, CAP), jnp.int32),
+            pltpu.VMEM((1, 1), jnp.int32),
             pltpu.VMEM((4096, LANES), F32), pltpu.VMEM((1024, 512), BF16),
             pltpu.VMEM((512, LANES), F32), pltpu.VMEM((4096, LANES), F32),
             pltpu.VMEM((384, LANES), F32), pltpu.VMEM((384, LANES), F32),
@@ -728,33 +728,34 @@
             pltpu.VMEM((6 * ELEMS, 512), BF16), pltpu.VMEM((256, 512), F32),
             pltpu.VMEM((LANES, LANES), F32), pltpu.VMEM((1024, 768), BF16),
             pltpu.VMEM((768, ELEMS), BF16), pltpu.VMEM((6 * 512, ELEMS), F32),
-            pltpu.SemaphoreType.DMA((11,)), pltpu.SemaphoreType.DMA((2,)),
+            pltpu.SemaphoreType.DMA((12,)), pltpu.SemaphoreType.DMA((2,)),
         ],
         compiler_params=params(30),
         cost_estimate=cost(10),
         name="volume",
     )(
-        x_view, velocity, metric, face_scale, deriv, face_partner, link, outlet_face, *received
+        x_view, velocity, metric, face_scale, deriv, face_partner, link, outlet_face,
+        elem_count.reshape(1, 1), *received
     )
 
     out, multiplier = pl.pallas_call(
         final_kernel,
         out_shape=(f32(32, 8, 16, LANES), f32(OBJ, 8)),
-        in_specs=[ANY] * 6 + [VMEM],
+        in_specs=[ANY] * 5 + [VMEM],
         out_specs=(ANY, VMEM),
         scratch_shapes=[
-            pltpu.VMEM((8, ELEMS), F32), pltpu.VMEM((4096, LANES), F32),
+            pltpu.VMEM((4096, LANES), F32),
             pltpu.VMEM((6, ELEMS), F32), pltpu.VMEM((LEVELS, 1, CAP), jnp.int32),
             pltpu.VMEM((1, CAP), jnp.int32), pltpu.VMEM((1, CAP), jnp.int32),
             pltpu.VMEM((32, 8, 16, LANES), F32),
             pltpu.VMEM((LANES, LANES), F32), pltpu.VMEM((48, ELEMS), F32),
             pltpu.VMEM((384, LANES), F32), pltpu.VMEM((CAP, LANES), F32),
-            pltpu.SemaphoreType.DMA((6,)), pltpu.SemaphoreType.DMA((8,)),
+            pltpu.SemaphoreType.DMA((5,)), pltpu.SemaphoreType.DMA((8,)),
         ],
         compiler_params=params(30),
         cost_estimate=cost(3),
         name="finish",
-    )(live, acc, face_scale, link, outlet_face, outlet_id, messages)
+    )(acc, face_scale, link, outlet_face, outlet_id, messages)
     out = (
         out.reshape(COMPS, OBJ, 8, 2, 8, LANES).transpose(0, 1, 2, 4, 3, 5)
         .reshape(COMPS, OBJ, NODES, ELEMS)

time: 49.7 us -> 49 us (0.986)
  waiting for transfers between devices: 3.28 us -> 2.6 us
    ppermute x7, waiting for transfers between devices: 3.27 us -> 2.6 us  [swap(): return lax.ppermute(block, 'dom', [(i, i ^ mask) for i in range(devices)])]
    unnamed x24 -> x22, local copies, waits for them, and re-layouts: 2.94 us -> 2.95 us
  transfers between devices with their start and end apart: 8 -> 8, of which waited for: 2 -> 1; matrix products, arithmetic and copies ran while one was open for 0% -> 0% of each run, Pallas kernels for 17% -> 18%
where the time goes in v1:
time: 49 us; the launch traced here: 48.8 us
  starting transfers between devices  24.2 us (49%)
  Pallas kernels  17.5 us (36%)
  local copies, waits for them, and re-layouts  2.95 us (6%)
  waiting for transfers between devices  2.6 us (5%)
  between operations  1.64 us (3%)
    ppermute x7, starting transfers between devices, swap(): return lax.ppermute(block, 'dom', [(i, i ^ mask) for i in range(devices)])  13 us
    all_to_all x1, starting transfers between devices, local(): lax.all_to_all(message.reshape(devices, MSG, LANES), 'dom', split_axis=0,...  11.2 us
    pallas_call x1, Pallas kernels, local(): pl.pallas_call(main_kernel, out_shape=f32(4096, LANES), in_specs=[ANY] *...  8.69 us
    pallas_call x1, Pallas kernels, local(): pl.pallas_call(gather_kernel, out_shape=(f32(devices * MSG, LANES),) + (f...  5.14 us
    pallas_call x1, Pallas kernels, local(): pl.pallas_call(final_kernel, out_shape=(f32(32, 8, 16, LANES), f32(OBJ, 8...  3.63 us
    unnamed x22, local copies, waits for them, and re-layouts  2.95 us
    ppermute x7, waiting for transfers between devices, swap(): return lax.ppermute(block, 'dom', [(i, i ^ mask) for i in range(devices)])  2.6 us
  transfers between devices with their start and end apart: 8, of which 1 were waited for; matrix products, arithmetic and copies ran while one was open for 0% of the time, Pallas kernels for 18%

profile of v1, /device:TPU:0, one launch (start us, length us, event | category | flops | bytes accessed | tf_op | source)
XLA Modules:
  0.0 48.8 jit_solution(1630149940371903729)
XLA Ops:
  0.6 0.0 copy-start.4
  0.6 0.0 copy-start.8
  0.7 0.0 copy-start.5
  0.7 0.0 copy-start.3
  0.7 0.0 copy-start.6
  0.7 0.0 copy-start
  0.7 0.0 copy-start.7
  0.7 0.0 copy-start.9
  0.7 5.1 %gather.1 = (f32[512,128]{1,0:T(8,128)}, f32[128,128]{1,0:T(8,128)}, f32[128,128]{1,0:T(8,128)}, f32[128,128]{1,0:T(8,128)}, f32[128,128]{1,0:T(8,128)}, /*index...) custom-call(f32[4096,128]{1,0:T(8,128)} %bitcast.15, bf16[3,64,256]{2,1,0:T(8,128)(2,1)} %vel_any.3, ...), custom_call_target="tpu_custom_call" | custom-call | flops 5000 | bytes 15000000 | tf_op jit(solution)/shard_map/gather/pallas_call | solution.py:682
  5.9 11.2 %all-to-all-start = ((f32[128,4,128]{2,1,0:T(4,128)}), f32[128,4,128]{2,1,0:T(4,128)S(1)}, u32[]{:S(2)}, u32[]{:S(2)}) async-start(f32[128,4,128]{2,1,0:T(4,128)} %bitcast.21), calls=%async_computation | async-start | bytes 524288 | tf_op jit(solution)/shard_map/all_to_all | solution.py:703
  17.1 0.1 collective-permute-start
  17.1 1.2 %collective-permute-start.1 = (f32[128,128]{1,0:T(8,128)}, f32[128,128]{1,0:T(8,128)S(1)}, u32[]{:S(2)}, u32[]{:S(2)}) collective-permute-start(f32[128,128]{1,0:T(8,128)} %get-tuple-element.13), channel_id=1, source_target_pairs={{0,2},{1,3},{2,0},{3,1},{4,6},{5,7},{6,4},{7,5},{8,10},{9,11},{10,... | collective-permute-start | bytes 196616 | tf_op jit(solution)/shard_map/ppermute | solution.py:708
  18.3 3.2 %collective-permute-start.2 = (f32[128,128]{1,0:T(8,128)}, f32[128,128]{1,0:T(8,128)S(1)}, u32[]{:S(2)}, u32[]{:S(2)}) collective-permute-start(f32[128,128]{1,0:T(8,128)} %get-tuple-element.14), channel_id=1, source_target_pairs={{0,4},{1,5},{2,6},{3,7},{4,0},{5,1},{6,2},{7,3},{8,12},{9,13},{10,... | collective-permute-start | bytes 196616 | tf_op jit(solution)/shard_map/ppermute | solution.py:708
  21.5 1.5 %collective-permute-start.3 = (f32[128,128]{1,0:T(8,128)}, f32[128,128]{1,0:T(8,128)S(1)}, u32[]{:S(2)}, u32[]{:S(2)}) collective-permute-start(f32[128,128]{1,0:T(8,128)} %get-tuple-element.15), channel_id=1, source_target_pairs={{0,8},{1,9},{2,10},{3,11},{4,12},{5,13},{6,14},{7,15},{8,0},{9,1},... | collective-permute-start | bytes 196616 | tf_op jit(solution)/shard_map/ppermute | solution.py:708
  23.1 2.8 %collective-permute-start.4 = (f32[128,128]{1,0:T(8,128)}, f32[128,128]{1,0:T(8,128)S(1)}, u32[]{:S(2)}, u32[]{:S(2)}) collective-permute-start(f32[128,128]{1,0:T(8,128)} %get-tuple-element.16), channel_id=1, source_target_pairs={{0,16},{1,17},{2,18},{3,19},{4,20},{5,21},{6,22},{7,23},{8,24},{9,... | collective-permute-start | bytes 196616 | tf_op jit(solution)/shard_map/ppermute | solution.py:708
  25.9 0.0 collective-permute-done.s0_ref
  25.9 1.5 %collective-permute-start.5 = (f32[128,128]{1,0:T(8,128)}, f32[128,128]{1,0:T(8,128)S(1)}, u32[]{:S(2)}, u32[]{:S(2)}) collective-permute-start(f32[128,128]{1,0:T(8,128)} %get-tuple-element.17), channel_id=1, source_target_pairs={{0,32},{1,33},{2,34},{3,35},{4,36},{5,37},{6,38},{7,39},{8,40},{9,... | collective-permute-start | bytes 196616 | tf_op jit(solution)/shard_map/ppermute | solution.py:708
  27.4 0.0 collective-permute-done.1.s1_ref
  27.4 2.7 %collective-permute-start.6 = (f32[128,128]{1,0:T(8,128)}, f32[128,128]{1,0:T(8,128)S(1)}, u32[]{:S(2)}, u32[]{:S(2)}) collective-permute-start(f32[128,128]{1,0:T(8,128)} %get-tuple-element.18), channel_id=1, source_target_pairs={{0,64},{1,65},{2,66},{3,67},{4,68},{5,69},{6,70},{7,71},{8,72},{9,... | collective-permute-start | bytes 196616 | tf_op jit(solution)/shard_map/ppermute | solution.py:708
  30.7 0.0 collective-permute-done.2.s2_ref
  30.7 0.0 collective-permute-done.3.s3_ref
  30.8 0.0 collective-permute-done.4.s4_ref
  30.8 0.0 collective-permute-done.5.s5_ref
  30.8 2.6 %collective-permute-done.6.s6_ref = f32[128,128]{1,0:T(8,128)S(1)} collective-permute-done((f32[128,128]{1,0:T(8,128)}, f32[128,128]{1,0:T(8,128)S(1)}, u32[]{:S(2)}, u32[]{:S(2)}) %collective-permute-start.6) | collective-permute-done | bytes 65568 | tf_op jit(solution)/shard_map/ppermute | solution.py:708
  33.4 0.0 copy-done.4
  33.4 0.0 copy-done.8
  33.4 0.0 copy-done.5
  33.4 0.0 copy-done.3
  33.4 0.0 copy-done.6
  33.4 0.0 copy-done
  33.4 0.0 copy-done.7
  33.4 0.0 copy-done.9
  33.4 0.0 copy-start.10
  33.4 8.7 %volume.1.acc_any = f32[4096,128]{1,0:T(8,128)S(1)} custom-call(f32[4096,128]{1,0:T(8,128)S(1)} %bitcast.16, bf16[3,64,256]{2,1,0:T(8,128)(2,1)S(1)} %copy-done.3, f32[3,256]{1,0:T(4,128)S(1)} %copy-done.9, f32[6,256]{1,0:T(8,128)S(1)} %copy-done.5, bf16[576,64]{1,0:T(8,128)(2,1)S(1)} %copy-done.4, s32[6,256]{1,0:T(8,128)S(1)} %copy-done.7, ...), custom_call_target="tpu_custom_call" | custom-call | flops 10000 | bytes 30000000 | tf_op jit(solution)/shard_map/volume/pallas_call | solution.py:713
  42.1 0.0 copy-start.1
  42.1 1.3 %copy-done.1 = f32[4096,128]{1,0:T(8,128)} copy-done((f32[4096,128]{1,0:T(8,128)}, f32[4096,128]{1,0:T(8,128)S(1)}, u32[]{:S(2)}) %copy-start.1) | copy-done | bytes 2097176
  43.4 0.0 all-to-all-done
  43.5 0.0 copy-done.10
  43.5 0.0 copy-start.2
  43.5 1.6 %copy-done.2 = f32[4096,128]{1,0:T(8,128)S(1)} copy-done((f32[4096,128]{1,0:T(8,128)S(1)}, f32[4096,128]{1,0:T(8,128)}, u32[]{:S(2)}) %copy-start.2) | copy-done | bytes 2097176
  45.0 3.6 %finish.1 = (f32[32,8,16,128]{3,2,1,0:T(8,128)}, f32[8,8]{1,0:T(8,128)}) custom-call(f32[4096,128]{1,0:T(8,128)S(1)} %copy-done.2, f32[6,256]{1,0:T(8,128)S(1)} %copy-done.5, s32[7,1,32]{2,1,0:T(1,128)S(1)} %bitcast.20, s32[1,32]{1,0:T(1,128)S(1)} %copy-done.8, s32[1,32]{1,0:T(1,128)S(1)} %copy-done.10, f32[512,128]{1,0:T(8,128)S(1)} %bitcast.17), custom_call_target="tpu_custom_call" | custom-call | flops 3000 | bytes 9000000 | tf_op jit(solution)/shard_map/finish/pallas_call | solution.py:741
Async XLA Ops:
  0.6 32.7 %copy-start.4 = (bf16[576,64]{1,0:T(8,128)(2,1)S(1)}, bf16[576,64]{1,0:T(8,128)(2,1)}, u32[]{:S(2)}) copy-start(bf16[576,64]{1,0:T(8,128)(2,1)} %constant.4.clone.deriv_any) | copy-start | bytes 221188
  0.6 32.7 %copy-start.8 = (s32[1,32]{1,0:T(1,128)S(1)}, s32[1,32]{1,0:T(1,128)}, u32[]{:S(2)}) copy-start(s32[1,32]{1,0:T(1,128)} %outlet_any.5) | copy-start | bytes 388
  0.7 32.7 %copy-start.5 = (f32[6,256]{1,0:T(8,128)S(1)}, f32[6,256]{1,0:T(8,128)}, u32[]{:S(2)}) copy-start(f32[6,256]{1,0:T(8,128)} %scale_any.5) | copy-start | bytes 18436
  0.7 32.7 %copy-start.3 = (bf16[3,64,256]{2,1,0:T(8,128)(2,1)S(1)}, bf16[3,64,256]{2,1,0:T(8,128)(2,1)}, u32[]{:S(2)}) copy-start(bf16[3,64,256]{2,1,0:T(8,128)(2,1)} %vel_any.3) | copy-start | bytes 294916
  0.7 32.7 %copy-start.6 = (s32[1,7,32]{2,0,1:T(1,128)S(1)}, s32[1,7,32]{2,0,1:T(1,128)}, u32[]{:S(2)}) copy-start(s32[1,7,32]{2,0,1:T(1,128)} %param.19) | copy-start | bytes 2692
  0.7 32.7 %copy-start = (f32[4,8,64,256]{3,2,1,0:T(8,128)S(1)}, f32[4,8,64,256]{3,2,1,0:T(8,128)}, u32[]{:S(2)}) copy-start(f32[4,8,64,256]{3,2,1,0:T(8,128)} %param.12) | copy-start | bytes 6291460
  0.7 32.7 %copy-start.7 = (s32[6,256]{1,0:T(8,128)S(1)}, s32[6,256]{1,0:T(8,128)}, u32[]{:S(2)}) copy-start(s32[6,256]{1,0:T(8,128)} %partner_any.1) | copy-start | bytes 18436
  0.7 32.7 %copy-start.9 = (f32[3,256]{1,0:T(4,128)S(1)}, f32[3,256]{1,0:T(4,128)}, u32[]{:S(2)}) copy-start(f32[3,256]{1,0:T(4,128)} %metric_any.1) | copy-start | bytes 9220
  5.9 37.6 %all-to-all-start = ((f32[128,4,128]{2,1,0:T(4,128)}), f32[128,4,128]{2,1,0:T(4,128)S(1)}, u32[]{:S(2)}, u32[]{:S(2)}) async-start(f32[128,4,128]{2,1,0:T(4,128)} %bitcast.21), calls=%async_computation | async-start | bytes 524288 | tf_op jit(solution)/shard_map/all_to_all | solution.py:703
  17.1 8.8 %collective-permute-start = (f32[128,128]{1,0:T(8,128)}, f32[128,128]{1,0:T(8,128)S(1)}, u32[]{:S(2)}, u32[]{:S(2)}) collective-permute-start(f32[128,128]{1,0:T(8,128)} %get-tuple-element.12), channel_id=1, source_target_pairs={{0,1},{1,0},{2,3},{3,2},{4,5},{5,4},{6,7},{7,6},{8,9},{9,8},{10,11... | collective-permute-start | bytes 196616 | tf_op jit(solution)/shard_map/ppermute | solution.py:708
  17.1 10.2 %collective-permute-start.1 = (f32[128,128]{1,0:T(8,128)}, f32[128,128]{1,0:T(8,128)S(1)}, u32[]{:S(2)}, u32[]{:S(2)}) collective-permute-start(f32[128,128]{1,0:T(8,128)} %get-tuple-element.13), channel_id=1, source_target_pairs={{0,2},{1,3},{2,0},{3,1},{4,6},{5,7},{6,4},{7,5},{8,10},{9,11},{10,... | collective-permute-start | bytes 196616 | tf_op jit(solution)/shard_map/ppermute | solution.py:708
  18.3 12.4 %collective-permute-start.2 = (f32[128,128]{1,0:T(8,128)}, f32[128,128]{1,0:T(8,128)S(1)}, u32[]{:S(2)}, u32[]{:S(2)}) collective-permute-start(f32[128,128]{1,0:T(8,128)} %get-tuple-element.14), channel_id=1, source_target_pairs={{0,4},{1,5},{2,6},{3,7},{4,0},{5,1},{6,2},{7,3},{8,12},{9,13},{10,... | collective-permute-start | bytes 196616 | tf_op jit(solution)/shard_map/ppermute | solution.py:708
  21.5 9.2 %collective-permute-start.3 = (f32[128,128]{1,0:T(8,128)}, f32[128,128]{1,0:T(8,128)S(1)}, u32[]{:S(2)}, u32[]{:S(2)}) collective-permute-start(f32[128,128]{1,0:T(8,128)} %get-tuple-element.15), channel_id=1, source_target_pairs={{0,8},{1,9},{2,10},{3,11},{4,12},{5,13},{6,14},{7,15},{8,0},{9,1},... | collective-permute-start | bytes 196616 | tf_op jit(solution)/shard_map/ppermute | solution.py:708
  23.1 7.7 %collective-permute-start.4 = (f32[128,128]{1,0:T(8,128)}, f32[128,128]{1,0:T(8,128)S(1)}, u32[]{:S(2)}, u32[]{:S(2)}) collective-permute-start(f32[128,128]{1,0:T(8,128)} %get-tuple-element.16), channel_id=1, source_target_pairs={{0,16},{1,17},{2,18},{3,19},{4,20},{5,21},{6,22},{7,23},{8,24},{9,... | collective-permute-start | bytes 196616 | tf_op jit(solution)/shard_map/ppermute | solution.py:708
  25.9 4.9 %collective-permute-start.5 = (f32[128,128]{1,0:T(8,128)}, f32[128,128]{1,0:T(8,128)S(1)}, u32[]{:S(2)}, u32[]{:S(2)}) collective-permute-start(f32[128,128]{1,0:T(8,128)} %get-tuple-element.17), channel_id=1, source_target_pairs={{0,32},{1,33},{2,34},{3,35},{4,36},{5,37},{6,38},{7,39},{8,40},{9,... | collective-permute-start | bytes 196616 | tf_op jit(solution)/shard_map/ppermute | solution.py:708
  27.4 6.0 %collective-permute-start.6 = (f32[128,128]{1,0:T(8,128)}, f32[128,128]{1,0:T(8,128)S(1)}, u32[]{:S(2)}, u32[]{:S(2)}) collective-permute-start(f32[128,128]{1,0:T(8,128)} %get-tuple-element.18), channel_id=1, source_target_pairs={{0,64},{1,65},{2,66},{3,67},{4,68},{5,69},{6,70},{7,71},{8,72},{9,... | collective-permute-start | bytes 196616 | tf_op jit(solution)/shard_map/ppermute | solution.py:708
  33.4 10.0 %copy-start.10 = (s32[1,32]{1,0:T(1,128)S(1)}, s32[1,32]{1,0:T(1,128)}, u32[]{:S(2)}) copy-start(s32[1,32]{1,0:T(1,128)} %ids_any.3) | copy-start | bytes 388
  42.1 1.3 %copy-start.1 = (f32[4096,128]{1,0:T(8,128)}, f32[4096,128]{1,0:T(8,128)S(1)}, u32[]{:S(2)}) copy-start(f32[4096,128]{1,0:T(8,128)S(1)} %volume.1.acc_any) | copy-start | bytes 6291460
  43.5 1.6 %copy-start.2 = (f32[4096,128]{1,0:T(8,128)S(1)}, f32[4096,128]{1,0:T(8,128)}, u32[]{:S(2)}) copy-start(f32[4096,128]{1,0:T(8,128)} %copy-done.1) | copy-start | bytes 6291460
